TPU v7x, 32 devices: a whole 2x2x4 slice. The times are simulated.
32 devices in a mesh: groups: 2 (over y), seq: 4 (over z), head: 2 (over x), sub: 2 (over core).
Axes of the slice: x: 2, y: 2, z: 4, core: 2. Of those that a mesh axis runs over, the one named last changes fastest.
Arguments:
- queries: bfloat16 [4608, 8192], P(('groups', 'seq'), ('head', 'sub')), parts along dimension 0, may hold values from -6 to 6
- keys: bfloat16 [4608, 8192], P(('groups', 'seq'), ('head', 'sub')), parts along dimension 0, may hold values from -0.0546875 to 0.0546875
- values: bfloat16 [4608, 8192], P(('groups', 'seq'), ('head', 'sub')), parts along dimension 0, may hold values from -800 to 800
- decay_exp: int32 [64], P(('head', 'sub')), may hold values from 1 to 2303, as said below
- gain: float32 [8192], P(('head', 'sub')), may hold values from 0.5 to 1.5
Outputs:
- normed: bfloat16 [4608, 8192], P(('groups', 'seq'), ('head', 'sub')), parts along dimension 0
- final_state: float32 [128, 128, 128], P(('groups', 'head', 'sub'), 'seq'), parts along dimension 0
There are 2 independent parts, one for each index of `groups`. A program takes and returns all parts, laid end to end along the dimension named above; an argument that names none is the same for every part. Nothing has to cross between parts.
Inputs may be any that keep to these rules, and one draw needn't show every extreme that they name: The decay of head h over one position is 2 ** (-decay_exp[h] / 18432).
All inputs are finite; a program needn't handle non-finite values.
Results may differ from a plain program's by a relative error of at most 0.0049.
Values sent between devices are 32-bit elements; how exact they have to be, the bound alone decides.
A program may use at most 64 MiB of HBM per device.

v0:
```python
import jax
import jax.numpy as jnp
from jax import lax
from jax.sharding import PartitionSpec as P

HEADS = 64
DK = 128


def local(queries, keys, values, decay_exp, gain):
    tokens = queries.shape[0]
    heads_here = decay_exp.shape[0]
    head_size = queries.shape[1] // heads_here
    n_seq = lax.axis_size("seq")
    decay_rate = decay_exp.astype(jnp.float32) / (8.0 * tokens * n_seq)
    offsets = jnp.arange(tokens).astype(jnp.float32)
    distance = offsets[:, None] - offsets[None, :]
    causal = distance >= 0
    within = jnp.where(
        causal[None], jnp.exp2(-decay_rate[:, None, None] * jnp.maximum(distance, 0.0)[None]), 0.0
    )
    key_decay = jnp.exp2(-decay_rate[None, :] * (tokens - 1.0 - offsets)[:, None])
    query_decay = jnp.exp2(-decay_rate[None, :] * (offsets + 1.0)[:, None])
    query_heads = queries.reshape(tokens, heads_here, head_size)
    key_heads = keys.reshape(tokens, heads_here, head_size)
    value_heads = values.reshape(tokens, heads_here, head_size)
    scaled_keys = (key_heads.astype(jnp.float32) * key_decay[:, :, None]).astype(jnp.bfloat16)
    local_state = jnp.einsum(
        "ihd,ihe->hde", scaled_keys, value_heads, preferred_element_type=jnp.float32
    )
    row_pieces = lax.all_to_all(local_state[None], "seq", split_axis=2, concat_axis=0, tiled=True)
    ranks = jnp.arange(n_seq).astype(jnp.float32)
    gap = ranks[:, None] - 1.0 - ranks[None, :]
    prior = jnp.where(
        gap[:, :, None] >= 0,
        jnp.exp2(-decay_rate[None, None, :] * tokens * jnp.maximum(gap, 0.0)[:, :, None]),
        0.0,
    )
    toward_end = jnp.exp2(-decay_rate[None, :] * tokens * (n_seq - 1.0 - ranks)[:, None])
    prefix_by_block = jnp.einsum(
        "bmh,mhre->bhre", prior, row_pieces, precision=lax.Precision.HIGHEST
    )
    final_rows = jnp.einsum("mh,mhre->hre", toward_end, row_pieces, precision=lax.Precision.HIGHEST)
    prefix = lax.all_to_all(prefix_by_block, "seq", split_axis=0, concat_axis=2, tiled=True)[0]
    scores = jnp.einsum("ihd,jhd->hij", query_heads, key_heads, preferred_element_type=jnp.float32)
    weights = (scores * within).astype(jnp.bfloat16)
    intra = jnp.einsum("hij,jhd->ihd", weights, value_heads, preferred_element_type=jnp.float32)
    decayed_query = query_heads.astype(jnp.float32) * query_decay[:, :, None]
    inter = jnp.einsum("ihd,hde->ihe", decayed_query, prefix, precision=lax.Precision.HIGHEST)
    mixed = (intra + inter).reshape(tokens, heads_here * head_size)
    squares = jnp.sum(mixed * mixed, axis=1)
    summed = lax.psum(squares, ("head", "sub"))
    mean_square = summed / (HEADS * DK)
    normed = (mixed * lax.rsqrt(mean_square + 1e-06)[:, None] * gain[None, :]).astype(jnp.bfloat16)
    return (normed, final_rows)


def solution(mesh):
    return jax.shard_map(
        local,
        mesh=mesh,
        in_specs=(
            P(("groups", "seq"), ("head", "sub")),
            P(("groups", "seq"), ("head", "sub")),
            P(("groups", "seq"), ("head", "sub")),
            P(("head", "sub")),
            P(("head", "sub")),
        ),
        out_specs=(
            P(("groups", "seq"), ("head", "sub")),
            P(("groups", "head", "sub"), "seq", None),
        ),
        check_vma=False,
    )
```

profile of v0, /device:TPU:0, one launch (start us, length us, event | category | flops | bytes accessed | tf_op | source)
XLA Modules:
  0.0 92.8 jit_solution(15200276459177829985)
XLA Ops:
  0.6 0.0 copy-start
  0.7 0.8 broadcast_multiply_fusion
  1.5 0.1 multiply_exponential_fusion
  1.6 4.7 %fusion.30 = f32[1,16,128,128]{3,2,1,0:T(8,128)S(1)} fusion(f32[576,16]{0,1:T(8,128)S(1)} %get-tuple-element.3, bf16[576,2048]{1,0:T(8,128)(2,1)} %param.7, bf16[576,2048]{1,0:T(8,128)(2,1)} %param.6), kind=kOutput, calls=%fused_computation.30 | convolution fusion | flops 305528832 | bytes 5804032 | tf_op jit(solution)/shard_map/ihd,ihe->hde/dot_general | solution.py:28
  6.3 1.6 %copy.34 = f32[1,16,128,128]{3,1,0,2:T(8,128)} copy(f32[1,16,128,128]{3,2,1,0:T(8,128)S(1)} %fusion.30) | data formatting | bytes 2097152 | tf_op jit(solution)/shard_map/broadcast_in_dim | solution.py:31
  7.8 6.3 %all-to-all-start = ((f32[1,16,128,128]{3,1,0,2:T(8,128)}), f32[1,16,128,128]{3,1,0,2:T(8,128)S(1)}, u32[]{:S(2)}, u32[]{:S(2)}) async-start(f32[1,16,128,128]{3,1,0,2:T(8,128)} %copy.34), calls=%async_computation | async-start | bytes 2097152 | tf_op jit(solution)/shard_map/all_to_all | solution.py:31
  14.2 0.1 exponential_bitcast_fusion
  14.3 0.1 copy.42
  14.4 0.1 subtract_compare_fusion.1
  14.4 0.1 subtract_maximum_fusion.1
  14.5 1.1 %subtract_compare_fusion = pred[576,576]{1,0:T(8,128)(4,1)} fusion(f32[576]{0:T(1024)S(1)} %iota_convert_fusion), kind=kLoop, calls=%fused_computation.23 | loop fusion | flops 663552 | bytes 334080 | tf_op jit(solution)/shard_map/ge | solution.py:18
  15.6 1.3 %subtract_maximum_fusion = f32[576,576]{1,0:T(8,128)} fusion(f32[576]{0:T(1024)S(1)} %iota_convert_fusion), kind=kLoop, calls=%fused_computation.22 | loop fusion | flops 663552 | bytes 1329408 | tf_op jit(solution)/shard_map/max | solution.py:20
  16.9 23.1 %all-to-all-done = f32[1,16,128,128]{3,1,0,2:T(8,128)S(1)} async-done(((f32[1,16,128,128]{3,1,0,2:T(8,128)}), f32[1,16,128,128]{3,1,0,2:T(8,128)S(1)}, u32[]{:S(2)}, u32[]{:S(2)}) %all-to-all-start) | async-done | bytes 1048608 | tf_op jit(solution)/shard_map/all_to_all | solution.py:31
  39.9 2.5 %convolution_bitcast_fusion = f32[4,16,32,128]{3,0,2,1:T(4,128)S(1)} fusion(f32[1,16,4,32,128]{4,1,3,2,0:T(8,128)S(1)} %bitcast.93, f32[4,4]{1,0:T(4,128)S(1)} %subtract_maximum_fusion.1, f32[16]{0:T(128)S(1)} %get-tuple-element.4, pred[4,4]{1,0:T(4,128)(4,1)S(1)} %subtract_compare_fusion.1), kind=kOutput, calls=%fused_computation.31 | convolution fusion | flops 12583680 | bytes 2097296 | tf_op jit(solution)/shard_map/bmh,mhre->bhre/dot_general | solution.py:40
  42.4 1.1 %copy.37 = f32[4,16,32,128]{3,2,1,0:T(8,128)} copy(f32[4,16,32,128]{3,0,2,1:T(4,128)S(1)} %convolution_bitcast_fusion) | data formatting | bytes 2097152 | tf_op jit(solution)/shard_map/bmh,mhre->bhre/transpose | solution.py:40
  43.6 4.4 %all-to-all-start.1 = ((f32[4,16,32,128]{3,2,1,0:T(8,128)}), f32[4,16,32,128]{3,2,1,0:T(8,128)}, u32[]{:S(2)}, u32[]{:S(2)}) async-start(f32[4,16,32,128]{3,2,1,0:T(8,128)} %copy.37), calls=%async_computation.1 | async-start | bytes 2097152 | tf_op jit(solution)/shard_map/all_to_all | solution.py:44
  48.0 0.0 copy-done
  48.1 12.4 %fusion = f32[16,576,128]{2,1,0:T(8,128)} fusion(f32[576,576]{1,0:T(8,128)} %subtract_maximum_fusion, f32[16]{0:T(128)S(1)} %get-tuple-element.5, pred[576,576]{1,0:T(8,128)(4,1)} %subtract_compare_fusion, bf16[576,2048]{1,0:T(8,128)(2,1)} %param.7, bf16[576,2048]{1,0:T(8,128)(2,1)} %param.6, bf16[576,2048]{1,0:T(8,128)(2,1)S(1)} %copy-done), kind=kOutput, calls=%fused_computation.1 | convolution fusion | flops 2744451072 | bytes 13455424 | tf_op jit(solution)/shard_map/hij,jhd->ihd/dot_general | solution.py:47
  60.5 3.1 %fusion.33 = f32[16,1,32,128]{3,1,2,0:T(1,128)} fusion(f32[4,16,1,1]{0,2,3,1:T(1,128)S(1)} %copy.42, f32[1,16,4,32,128]{4,1,3,2,0:T(8,128)S(1)} %bitcast.94), kind=kOutput, calls=%fused_computation.32 | convolution fusion | flops 3145728 | bytes 1310976 | tf_op jit(solution)/shard_map/mh,mhre->hre/dot_general | solution.py:43
  63.6 9.6 %all-to-all-done.1 = f32[4,16,32,128]{3,2,1,0:T(8,128)} async-done(((f32[4,16,32,128]{3,2,1,0:T(8,128)}), f32[4,16,32,128]{3,2,1,0:T(8,128)}, u32[]{:S(2)}, u32[]{:S(2)}) %all-to-all-start.1) | async-done | bytes 1048608 | tf_op jit(solution)/shard_map/all_to_all | solution.py:44
  73.2 1.3 %copy.38 = f32[4,16,32,128]{3,2,0,1:T(8,128)S(1)} copy(f32[4,16,32,128]{3,2,1,0:T(8,128)} %all-to-all-done.1) | data formatting | bytes 2097152 | tf_op jit(solution)/shard_map/all_to_all | solution.py:44
  74.5 0.0 copy-start.1
  74.5 8.2 %multiply_reduce_fusion = (f32[576]{0:T(1024)S(1)}, f32[576,16,128]{2,0,1:T(8,128)}) fusion(f32[16,128,128]{2,1,0:T(8,128)S(1)} %bitcast.95, f32[576,16]{0,1:T(8,128)S(1)} %get-tuple-element.2, f32[16,576,128]{2,1,0:T(8,128)} %fusion, bf16[576,2048]{1,0:T(8,128)(2,1)S(1)} %copy-done), kind=kOutput, calls=%fused_computation.8 | convolution fusion | flops 1817837056 | bytes 12884224 | tf_op jit(solution)/shard_map/ihd,hde->ihe/dot_general | solution.py:49
  82.7 5.8 %psum.7 = f32[576]{0:T(1024)S(1)} all-reduce(f32[576]{0:T(1024)S(1)} %get-tuple-element.6), channel_id=1, replica_groups=mesh['groups'=2,'seq'=4,'head'=2,'sub'=2] {'head','sub'}, use_global_device_ids=true, to_apply=%region_1.2 | all-reduce | flops 576 | bytes 4608 | tf_op jit(solution)/shard_map/psum | solution.py:52
  88.6 0.0 copy-done.1
  88.6 4.2 %fusion.5 = bf16[576,2048]{1,0:T(8,128)(2,1)} fusion(f32[2048]{0:T(1024)S(1)} %copy-done.1, f32[576]{0:T(1024)S(1)} %add_rsqrt_fusion, f32[576,16,128]{2,0,1:T(8,128)} %get-tuple-element.7), kind=kLoop, calls=%fused_computation.6 | loop fusion | flops 3538944 | bytes 7088384 | tf_op jit(solution)/shard_map/convert_element_type | solution.py:54
  (6 shorter events, 0.0 us)
Async XLA Ops:
  0.6 47.4 %copy-start = (bf16[576,2048]{1,0:T(8,128)(2,1)S(1)}, bf16[576,2048]{1,0:T(8,128)(2,1)}, u32[]{:S(2)}) copy-start(bf16[576,2048]{1,0:T(8,128)(2,1)} %param.5) | copy-start | bytes 7077892
  7.8 32.1 %all-to-all-start = ((f32[1,16,128,128]{3,1,0,2:T(8,128)}), f32[1,16,128,128]{3,1,0,2:T(8,128)S(1)}, u32[]{:S(2)}, u32[]{:S(2)}) async-start(f32[1,16,128,128]{3,1,0,2:T(8,128)} %copy.34), calls=%async_computation | async-start | bytes 2097152 | tf_op jit(solution)/shard_map/all_to_all | solution.py:31
  43.6 29.6 %all-to-all-start.1 = ((f32[4,16,32,128]{3,2,1,0:T(8,128)}), f32[4,16,32,128]{3,2,1,0:T(8,128)}, u32[]{:S(2)}, u32[]{:S(2)}) async-start(f32[4,16,32,128]{3,2,1,0:T(8,128)} %copy.37), calls=%async_computation.1 | async-start | bytes 2097152 | tf_op jit(solution)/shard_map/all_to_all | solution.py:44
  74.5 14.1 %copy-start.1 = (f32[2048]{0:T(1024)S(1)}, f32[2048]{0:T(1024)}, u32[]{:S(2)}) copy-start(f32[2048]{0:T(1024)} %param.9) | copy-start | bytes 24580
where the time goes:
time: 93.2 us; the launch traced here: 92.8 us
  waiting for transfers between devices  32.7 us (35%)
  matrix products  31 us (33%)
  starting transfers between devices  10.8 us (12%)
  other arithmetic  7.7 us (8%)
  blocking collectives  5.83 us (6%)
  local copies, waits for them, and re-layouts  4.14 us (4%)
    all_to_all x1, waiting for transfers between devices, local(): lax.all_to_all(local_state[None], 'seq', split_axis=2, concat_axis=0, til...  23.1 us
    dot_general x1, matrix products, local(): jnp.einsum('hij,jhd->ihd', weights, value_heads, preferred_element_type=j...  12.4 us
    all_to_all x1, waiting for transfers between devices, local(): lax.all_to_all(prefix_by_block, 'seq', split_axis=0, concat_axis=2, tiled...  9.61 us
    dot_general x1, matrix products, local(): jnp.einsum('ihd,hde->ihe', decayed_query, prefix, precision=lax.Precision...  8.2 us
    all_to_all x1, starting transfers between devices, local(): lax.all_to_all(local_state[None], 'seq', split_axis=2, concat_axis=0, til...  6.35 us
    psum x1, blocking collectives, local(): summed = lax.psum(squares, ('head', 'sub'))  5.83 us
    dot_general x1, matrix products, local(): jnp.einsum('ihd,ihe->hde', scaled_keys, value_heads, preferred_element_ty...  4.7 us
    all_to_all x1, starting transfers between devices, local(): lax.all_to_all(prefix_by_block, 'seq', split_axis=0, concat_axis=2, tiled...  4.44 us
  transfers between devices with their start and end apart: 2, of which 2 were waited for; matrix products, arithmetic and copies ran while one was open for 20% of the time, Pallas kernels for 0%

commit v1 on v0

--- a/solution.py
+++ b/solution.py
@@ -49,7 +49,7 @@
     inter = jnp.einsum("ihd,hde->ihe", decayed_query, prefix, precision=lax.Precision.HIGHEST)
     mixed = (intra + inter).reshape(tokens, heads_here * head_size)
     squares = jnp.sum(mixed * mixed, axis=1)
-    summed = lax.psum(squares, ("head", "sub"))
+    summed = lax.psum(lax.psum(squares, "head"), "sub")
     mean_square = summed / (HEADS * DK)
     normed = (mixed * lax.rsqrt(mean_square + 1e-06)[:, None] * gain[None, :]).astype(jnp.bfloat16)
     return (normed, final_rows)

time: 93.2 us -> 94.7 us (1.016)
  blocking collectives: 5.83 us -> 7.35 us
    psum x1 -> x2, blocking collectives: 5.83 us -> 7.35 us  [local(): summed = lax.psum(lax.psum(squares, 'head'), 'sub')]
  transfers between devices with their start and end apart: 2 -> 2, of which waited for: 2 -> 2; matrix products, arithmetic and copies ran while one was open for 20% -> 19% of each run, Pallas kernels for 0% -> 0%
where the time goes in v1:
time: 94.7 us; the launch traced here: 94.3 us
  waiting for transfers between devices  32.7 us (35%)
  matrix products  31 us (33%)
  starting transfers between devices  10.8 us (11%)
  other arithmetic  7.69 us (8%)
  blocking collectives  7.35 us (8%)
  local copies, waits for them, and re-layouts  4.14 us (4%)
    all_to_all x1, waiting for transfers between devices, local(): lax.all_to_all(local_state[None], 'seq', split_axis=2, concat_axis=0, til...  23.1 us
    dot_general x1, matrix products, local(): jnp.einsum('hij,jhd->ihd', weights, value_heads, preferred_element_type=j...  12.4 us
    all_to_all x1, waiting for transfers between devices, local(): lax.all_to_all(prefix_by_block, 'seq', split_axis=0, concat_axis=2, tiled...  9.61 us
    dot_general x1, matrix products, local(): jnp.einsum('ihd,hde->ihe', decayed_query, prefix, precision=lax.Precision...  8.19 us
    psum x2, blocking collectives, local(): summed = lax.psum(lax.psum(squares, 'head'), 'sub')  7.35 us
    all_to_all x1, starting transfers between devices, local(): lax.all_to_all(local_state[None], 'seq', split_axis=2, concat_axis=0, til...  6.35 us
    dot_general x1, matrix products, local(): jnp.einsum('ihd,ihe->hde', scaled_keys, value_heads, preferred_element_ty...  4.7 us
    all_to_all x1, starting transfers between devices, local(): lax.all_to_all(prefix_by_block, 'seq', split_axis=0, concat_axis=2, tiled...  4.42 us
  transfers between devices with their start and end apart: 2, of which 2 were waited for; matrix products, arithmetic and copies ran while one was open for 19% of the time, Pallas kernels for 0%

profile of v1, /device:TPU:0, one launch (start us, length us, event | category | flops | bytes accessed | tf_op | source)
XLA Modules:
  0.0 94.3 jit_solution(12664539737977755677)
XLA Ops:
  0.6 0.0 copy-start
  0.7 0.8 broadcast_multiply_fusion
  1.5 0.1 multiply_exponential_fusion
  1.6 4.7 %fusion.30 = f32[1,16,128,128]{3,2,1,0:T(8,128)S(1)} fusion(f32[576,16]{0,1:T(8,128)S(1)} %get-tuple-element.3, bf16[576,2048]{1,0:T(8,128)(2,1)} %param.7, bf16[576,2048]{1,0:T(8,128)(2,1)} %param.6), kind=kOutput, calls=%fused_computation.30 | convolution fusion | flops 305528832 | bytes 5804032 | tf_op jit(solution)/shard_map/ihd,ihe->hde/dot_general | solution.py:28
  6.3 1.6 %copy.34 = f32[1,16,128,128]{3,1,0,2:T(8,128)} copy(f32[1,16,128,128]{3,2,1,0:T(8,128)S(1)} %fusion.30) | data formatting | bytes 2097152 | tf_op jit(solution)/shard_map/broadcast_in_dim | solution.py:31
  7.9 6.3 %all-to-all-start = ((f32[1,16,128,128]{3,1,0,2:T(8,128)}), f32[1,16,128,128]{3,1,0,2:T(8,128)S(1)}, u32[]{:S(2)}, u32[]{:S(2)}) async-start(f32[1,16,128,128]{3,1,0,2:T(8,128)} %copy.34), calls=%async_computation | async-start | bytes 2097152 | tf_op jit(solution)/shard_map/all_to_all | solution.py:31
  14.2 0.1 exponential_bitcast_fusion
  14.3 0.1 copy.42
  14.4 0.1 subtract_compare_fusion.1
  14.5 0.1 subtract_maximum_fusion.1
  14.5 1.0 %subtract_compare_fusion = pred[576,576]{1,0:T(8,128)(4,1)} fusion(f32[576]{0:T(1024)S(1)} %iota_convert_fusion), kind=kLoop, calls=%fused_computation.23 | loop fusion | flops 663552 | bytes 334080 | tf_op jit(solution)/shard_map/ge | solution.py:18
  15.6 1.3 %subtract_maximum_fusion = f32[576,576]{1,0:T(8,128)} fusion(f32[576]{0:T(1024)S(1)} %iota_convert_fusion), kind=kLoop, calls=%fused_computation.22 | loop fusion | flops 663552 | bytes 1329408 | tf_op jit(solution)/shard_map/max | solution.py:20
  16.9 23.1 %all-to-all-done = f32[1,16,128,128]{3,1,0,2:T(8,128)S(1)} async-done(((f32[1,16,128,128]{3,1,0,2:T(8,128)}), f32[1,16,128,128]{3,1,0,2:T(8,128)S(1)}, u32[]{:S(2)}, u32[]{:S(2)}) %all-to-all-start) | async-done | bytes 1048608 | tf_op jit(solution)/shard_map/all_to_all | solution.py:31
  39.9 2.5 %convolution_bitcast_fusion = f32[4,16,32,128]{3,0,2,1:T(4,128)S(1)} fusion(f32[1,16,4,32,128]{4,1,3,2,0:T(8,128)S(1)} %bitcast.93, f32[4,4]{1,0:T(4,128)S(1)} %subtract_maximum_fusion.1, f32[16]{0:T(128)S(1)} %get-tuple-element.4, pred[4,4]{1,0:T(4,128)(4,1)S(1)} %subtract_compare_fusion.1), kind=kOutput, calls=%fused_computation.31 | convolution fusion | flops 12583680 | bytes 2097296 | tf_op jit(solution)/shard_map/bmh,mhre->bhre/dot_general | solution.py:40
  42.5 1.1 %copy.37 = f32[4,16,32,128]{3,2,1,0:T(8,128)} copy(f32[4,16,32,128]{3,0,2,1:T(4,128)S(1)} %convolution_bitcast_fusion) | data formatting | bytes 2097152 | tf_op jit(solution)/shard_map/bmh,mhre->bhre/transpose | solution.py:40
  43.6 4.4 %all-to-all-start.1 = ((f32[4,16,32,128]{3,2,1,0:T(8,128)}), f32[4,16,32,128]{3,2,1,0:T(8,128)}, u32[]{:S(2)}, u32[]{:S(2)}) async-start(f32[4,16,32,128]{3,2,1,0:T(8,128)} %copy.37), calls=%async_computation.1 | async-start | bytes 2097152 | tf_op jit(solution)/shard_map/all_to_all | solution.py:44
  48.0 0.0 copy-done
  48.0 12.4 %fusion = f32[16,576,128]{2,1,0:T(8,128)} fusion(f32[576,576]{1,0:T(8,128)} %subtract_maximum_fusion, f32[16]{0:T(128)S(1)} %get-tuple-element.5, pred[576,576]{1,0:T(8,128)(4,1)} %subtract_compare_fusion, bf16[576,2048]{1,0:T(8,128)(2,1)} %param.7, bf16[576,2048]{1,0:T(8,128)(2,1)} %param.6, bf16[576,2048]{1,0:T(8,128)(2,1)S(1)} %copy-done), kind=kOutput, calls=%fused_computation.1 | convolution fusion | flops 2744451072 | bytes 13455424 | tf_op jit(solution)/shard_map/hij,jhd->ihd/dot_general | solution.py:47
  60.5 3.1 %fusion.33 = f32[16,1,32,128]{3,1,2,0:T(1,128)} fusion(f32[4,16,1,1]{0,2,3,1:T(1,128)S(1)} %copy.42, f32[1,16,4,32,128]{4,1,3,2,0:T(8,128)S(1)} %bitcast.94), kind=kOutput, calls=%fused_computation.32 | convolution fusion | flops 3145728 | bytes 1310976 | tf_op jit(solution)/shard_map/mh,mhre->hre/dot_general | solution.py:43
  63.6 9.6 %all-to-all-done.1 = f32[4,16,32,128]{3,2,1,0:T(8,128)} async-done(((f32[4,16,32,128]{3,2,1,0:T(8,128)}), f32[4,16,32,128]{3,2,1,0:T(8,128)}, u32[]{:S(2)}, u32[]{:S(2)}) %all-to-all-start.1) | async-done | bytes 1048608 | tf_op jit(solution)/shard_map/all_to_all | solution.py:44
  73.2 1.3 %copy.38 = f32[4,16,32,128]{3,2,0,1:T(8,128)S(1)} copy(f32[4,16,32,128]{3,2,1,0:T(8,128)} %all-to-all-done.1) | data formatting | bytes 2097152 | tf_op jit(solution)/shard_map/all_to_all | solution.py:44
  74.5 0.0 copy-start.1
  74.5 8.2 %multiply_reduce_fusion = (f32[576]{0:T(1024)S(1)}, f32[576,16,128]{2,0,1:T(8,128)}) fusion(f32[16,128,128]{2,1,0:T(8,128)S(1)} %bitcast.95, f32[576,16]{0,1:T(8,128)S(1)} %get-tuple-element.2, f32[16,576,128]{2,1,0:T(8,128)} %fusion, bf16[576,2048]{1,0:T(8,128)(2,1)S(1)} %copy-done), kind=kOutput, calls=%fused_computation.8 | convolution fusion | flops 1817837056 | bytes 12884224 | tf_op jit(solution)/shard_map/ihd,hde->ihe/dot_general | solution.py:49
  82.7 4.9 %psum.14 = f32[576]{0:T(1024)S(1)} all-reduce(f32[576]{0:T(1024)S(1)} %get-tuple-element.6), channel_id=1, replica_groups=mesh['groups'=2,'seq'=4,'head'=2,'sub'=2] {'head'}, use_global_device_ids=true, to_apply=%region_1.2 | all-reduce | flops 576 | bytes 4608 | tf_op jit(solution)/shard_map/psum | solution.py:52
  87.6 2.4 %psum.15 = f32[576]{0:T(1024)S(1)} all-reduce(f32[576]{0:T(1024)S(1)} %psum.14), channel_id=1, replica_groups=mesh['groups'=2,'seq'=4,'head'=2,'sub'=2] {'sub'}, use_global_device_ids=true, to_apply=%region_2.3 | all-reduce | flops 576 | bytes 4608 | tf_op jit(solution)/shard_map/psum | solution.py:52
  90.1 0.0 copy-done.1
  90.1 4.2 %fusion.5 = bf16[576,2048]{1,0:T(8,128)(2,1)} fusion(f32[2048]{0:T(1024)S(1)} %copy-done.1, f32[576]{0:T(1024)S(1)} %add_rsqrt_fusion, f32[576,16,128]{2,0,1:T(8,128)} %get-tuple-element.7), kind=kLoop, calls=%fused_computation.6 | loop fusion | flops 3538944 | bytes 7088384 | tf_op jit(solution)/shard_map/convert_element_type | solution.py:54
  (6 shorter events, 0.0 us)
Async XLA Ops:
  0.6 47.4 %copy-start = (bf16[576,2048]{1,0:T(8,128)(2,1)S(1)}, bf16[576,2048]{1,0:T(8,128)(2,1)}, u32[]{:S(2)}) copy-start(bf16[576,2048]{1,0:T(8,128)(2,1)} %param.5) | copy-start | bytes 7077892
  7.9 32.1 %all-to-all-start = ((f32[1,16,128,128]{3,1,0,2:T(8,128)}), f32[1,16,128,128]{3,1,0,2:T(8,128)S(1)}, u32[]{:S(2)}, u32[]{:S(2)}) async-start(f32[1,16,128,128]{3,1,0,2:T(8,128)} %copy.34), calls=%async_computation | async-start | bytes 2097152 | tf_op jit(solution)/shard_map/all_to_all | solution.py:31
  43.6 29.6 %all-to-all-start.1 = ((f32[4,16,32,128]{3,2,1,0:T(8,128)}), f32[4,16,32,128]{3,2,1,0:T(8,128)}, u32[]{:S(2)}, u32[]{:S(2)}) async-start(f32[4,16,32,128]{3,2,1,0:T(8,128)} %copy.37), calls=%async_computation.1 | async-start | bytes 2097152 | tf_op jit(solution)/shard_map/all_to_all | solution.py:44
  74.5 15.6 %copy-start.1 = (f32[2048]{0:T(1024)S(1)}, f32[2048]{0:T(1024)}, u32[]{:S(2)}) copy-start(f32[2048]{0:T(1024)} %param.9) | copy-start | bytes 24580
